TPU v7x, 32 devices: a whole 2x2x4 slice. The times are simulated.
32 devices in a mesh: groups: 2 (over y), seq: 4 (over z), dp: 4 (over x, core).
Axes of the slice: x: 2, y: 2, z: 4, core: 2. Of those that a mesh axis runs over, the one named last changes fastest.
Arguments:
- inputs: bfloat16 [8, 32768, 768], P(('groups', 'dp'), 'seq'), parts along dimension 0, may hold values from -33 to 33, as said below
- norm_gain: float32 [768], replicated, may hold values from 0.5 to 1.5
- inner_mix: bfloat16 [256, 256], replicated, may hold values from -0.375 to 0.375
- twiddle: float32 [128, 256], P('seq'), may hold values from 0.5 to 2
- outer_mix: bfloat16 [128, 128], replicated, may hold values from -0.5 to 0.5
- long_kernel: float32 [128, 256], P(None, 'seq'), may hold values from 0.5 to 2
- gate_weight: bfloat16 [768, 384], replicated, may hold values from -0.3125 to 0.3125
- out_weight: bfloat16 [768, 384], replicated, may hold values from -0.3125 to 0.3125
- cotangent: bfloat16 [8, 32768, 768], P(('groups', 'dp'), 'seq'), parts along dimension 0, may hold values from -6 to 6
Outputs:
- layer_out: bfloat16 [8, 32768, 768], P(('groups', 'dp'), 'seq'), parts along dimension 0
- input_grad: bfloat16 [8, 32768, 768], P(('groups', 'dp'), 'seq'), parts along dimension 0
- weight_grads: float32 [3072, 384], P(('groups', 'seq')), parts along dimension 0
There are 2 independent parts, one for each index of `groups`. A program takes and returns all parts, laid end to end along the dimension named above; an argument that names none is the same for every part. Nothing has to cross between parts.
Inputs may be any that keep to these rules, and one draw needn't show every extreme that they name: `inputs`: activations' entries.
All inputs are finite; a program needn't handle non-finite values.
Results may differ from a plain program's by a relative error of at most 0.0072.
Values may be sent and summed in bfloat16 or wider, within the bound.
A program may use at most 384 MiB of HBM per device.

v0:
```python
import math
import jax
import jax.numpy as jnp
from jax import lax
from jax.sharding import PartitionSpec as P

norm_eps = 1e-06


def normalize(values, norm_gain):
    mean_square = jnp.mean(values * values, axis=-1, keepdims=True)
    return values * lax.rsqrt(mean_square + norm_eps) * norm_gain


def block_apply(operand, weight):
    blocks = weight.shape[0] // weight.shape[1]
    grouped = operand.reshape(operand.shape[0], blocks, weight.shape[1])
    stacked = weight.reshape(blocks, weight.shape[1], weight.shape[1])
    result = jnp.einsum("rki,kij->rkj", grouped, stacked, preferred_element_type=jnp.float32)
    return result.reshape(operand.shape[0], -1)


def block_back(partner, weight):
    blocks = weight.shape[0] // weight.shape[1]
    grouped = partner.reshape(partner.shape[0], blocks, weight.shape[1])
    stacked = weight.reshape(blocks, weight.shape[1], weight.shape[1])
    result = jnp.einsum("rkj,kij->rki", grouped, stacked, preferred_element_type=jnp.float32)
    return result.reshape(partner.shape[0], -1)


def block_term(operand, partner, blocks, block_size):
    grouped = operand.reshape(operand.shape[0], blocks, block_size)
    other_rows = partner.reshape(partner.shape[0], blocks, block_size)
    result = jnp.einsum("rki,rkj->kij", grouped, other_rows, preferred_element_type=jnp.float32)
    return result.reshape(blocks * block_size, block_size)


def to_columns(row_layout):
    return lax.all_to_all(row_layout, "seq", split_axis=2, concat_axis=1, tiled=True)


def to_rows(col_layout):
    return lax.all_to_all(col_layout, "seq", split_axis=1, concat_axis=2, tiled=True)


def shards(
    inputs,
    norm_gain,
    inner_mix,
    twiddle,
    outer_mix,
    long_kernel,
    gate_weight,
    out_weight,
    cotangent,
):
    batch_local, rows_local, channels = inputs.shape
    inner_len = inner_mix.shape[0]
    local_outer = rows_local // inner_len
    flat_rows = batch_local * rows_local
    block_size = gate_weight.shape[1]
    blocks = gate_weight.shape[0] // block_size
    all_tokens = batch_local * lax.axis_size("dp") * rows_local * lax.axis_size("seq")
    grad_scale = 1.0 / math.sqrt(all_tokens)
    inputs_wide = inputs.reshape(flat_rows, channels).astype(jnp.float32)
    activation = normalize(inputs_wide, norm_gain).astype(jnp.bfloat16)
    grid_rows = activation.reshape(batch_local, local_outer, inner_len, channels)
    inner_out = jnp.einsum(
        "jq,bpqd->bpjd", inner_mix, grid_rows, preferred_element_type=jnp.float32
    )
    mixed_rows = (inner_out * twiddle[None, :, :, None]).astype(jnp.bfloat16)
    columns = to_columns(mixed_rows)
    outer_out = jnp.einsum("ip,bpjd->bijd", outer_mix, columns, preferred_element_type=jnp.float32)
    mixed_cols = (outer_out * long_kernel[None, :, :, None]).astype(jnp.bfloat16)
    seq_mix = to_rows(mixed_cols).reshape(flat_rows, channels)
    gate_pre = block_apply(activation, gate_weight)
    gate_sig = jax.nn.sigmoid(gate_pre)
    mix_wide = seq_mix.astype(jnp.float32)
    gated_rows = (mix_wide * gate_pre * gate_sig).astype(jnp.bfloat16)
    layer_out = (inputs_wide + block_apply(gated_rows, out_weight)).astype(jnp.bfloat16)
    cotan_rows = cotangent.reshape(flat_rows, channels)
    back_gated = block_back(cotan_rows, out_weight)
    mix_grad = (back_gated * gate_pre * gate_sig).astype(jnp.bfloat16)
    gate_grad = (back_gated * mix_wide * gate_sig * (1.0 + gate_pre * (1.0 - gate_sig))).astype(
        jnp.bfloat16
    )
    act_grad = block_back(gate_grad, gate_weight)
    weight_term = jnp.concatenate(
        [
            block_term(activation, gate_grad, blocks, block_size),
            block_term(gated_rows, cotan_rows, blocks, block_size),
        ],
        axis=0,
    )
    grad_cols = to_columns(mix_grad.reshape(batch_local, local_outer, inner_len, channels))
    scaled_back = (grad_cols.astype(jnp.float32) * long_kernel[None, :, :, None]).astype(
        jnp.bfloat16
    )
    back_outer = jnp.einsum(
        "ip,bijd->bpjd", outer_mix, scaled_back, preferred_element_type=jnp.float32
    ).astype(jnp.bfloat16)
    back_rows = to_rows(back_outer)
    twisted = (back_rows.astype(jnp.float32) * twiddle[None, :, :, None]).astype(jnp.bfloat16)
    inner_back = jnp.einsum("jq,bpjd->bpqd", inner_mix, twisted, preferred_element_type=jnp.float32)
    act_grad = act_grad + inner_back.reshape(flat_rows, channels)
    pullback = jax.vjp(lambda wide_rows: normalize(wide_rows, norm_gain), inputs_wide)[1]
    input_grad = (cotan_rows.astype(jnp.float32) + pullback(act_grad)[0]).astype(jnp.bfloat16)
    shard_term = lax.psum_scatter(weight_term, "seq", scatter_dimension=0, tiled=True)
    weight_grads = lax.psum(shard_term, "dp") * grad_scale
    return (layer_out.reshape(inputs.shape), input_grad.reshape(inputs.shape), weight_grads)


def solution(mesh):
    return jax.shard_map(
        shards,
        mesh=mesh,
        in_specs=(
            P(("groups", "dp"), "seq", None),
            P(),
            P(),
            P("seq", None),
            P(),
            P(None, "seq"),
            P(),
            P(),
            P(("groups", "dp"), "seq", None),
        ),
        out_specs=(
            P(("groups", "dp"), "seq", None),
            P(("groups", "dp"), "seq", None),
            P(("groups", "seq"), None),
        ),
        check_vma=False,
    )
```

profile of v0, /device:TPU:21, one launch (start us, length us, event | category | flops | bytes accessed | tf_op | source)
XLA Modules:
  0.0 1638.3 jit_solution(11999235351812838798)
XLA Ops:
  7.2 0.0 copy-start
  7.2 7.2 fusion.21
  14.4 0.0 copy-start.10
  14.4 14.3 convert_element_type.135
  28.7 0.0 copy-start.6
  28.7 0.0 copy-start.8
  28.7 0.0 copy-start.18
  28.8 24.7 %copy.107 = f32[32,256,768]{1,2,0:T(8,128)} copy(f32[32,256,768]{2,1,0:T(8,128)} %bitcast.156) | data formatting | bytes 50331648 | tf_op jit(solution)/shard_map/convert_element_type | solution.py:65
  53.5 0.0 copy-done.8
  53.5 14.2 fusion.24
  67.6 16.6 %copy.108 = bf16[1,32,256,768]{3,1,0,2:T(8,128)(2,1)} copy(bf16[1,32,256,768]{2,3,1,0:T(8,128)(2,1)} %fusion.24) | data formatting | bytes 25165824 | tf_op jit(solution)/shard_map/convert_element_type | solution.py:71
  84.2 275.7 %all_to_all.42 = bf16[1,32,256,768]{3,1,0,2:T(8,128)(2,1)S(1)} all-to-all(bf16[1,32,256,768]{3,1,0,2:T(8,128)(2,1)} %copy.108), channel_id=1, replica_groups=mesh['groups'=2,'seq'=4,'dp'=4] {'seq'}, dimensions={2} | all-to-all | bytes 25165824 | tf_op jit(solution)/shard_map/all_to_all | solution.py:39
  359.9 16.4 %copy.109 = bf16[1,32,256,768]{3,2,1,0:T(8,128)(2,1)S(1)} copy(bf16[1,32,256,768]{3,1,0,2:T(8,128)(2,1)S(1)} %all_to_all.42) | data formatting | bytes 25165824 | tf_op jit(solution)/shard_map/all_to_all | solution.py:39
  376.4 5.3 copy.110
  381.6 0.0 copy-done.12
  381.6 24.2 %fusion.7 = bf16[1,128,64,768]{1,3,2,0:T(8,128)(2,1)} fusion(f32[128,64]{0,1:T(8,128)S(1)} %copy-done.12, bf16[128,64,768]{2,1,0:T(8,128)(2,1)} %bitcast.157, bf16[128,128]{1,0:T(8,128)(2,1)S(1)} %copy-done.16), kind=kOutput, calls=%fused_computation.14 | convolution fusion | flops 1623195648 | bytes 25231360 | tf_op jit(solution)/shard_map/ip,bpjd->bijd/dot_general | solution.py:73
  405.8 16.5 %copy.112 = bf16[1,128,64,768]{3,2,0,1:T(8,128)(2,1)} copy(bf16[1,128,64,768]{1,3,2,0:T(8,128)(2,1)} %fusion.7) | data formatting | bytes 25165824 | tf_op jit(solution)/shard_map/convert_element_type | solution.py:74
  422.3 8.0 all-to-all-start.1
  430.3 0.0 copy-start.14
  430.3 0.0 copy-start.4
  430.4 17.6 %copy.142 = f32[1,8192,768]{1,2,0:T(8,128)} copy(bf16[1,8192,768]{2,1,0:T(8,128)(2,1)} %param.9) | data formatting | bytes 37748736 | tf_op jit(solution)/shard_map/convert_element_type | solution.py:65
  448.0 24.3 %reshape_reshape.4 = bf16[8192,2,384]{2,1,0:T(2,128)(2,1)} reshape(bf16[1,8192,768]{2,1,0:T(8,128)(2,1)} %param.17) | data formatting | bytes 25165824 | tf_op jit(solution)/shard_map/reshape;reshape | solution.py:25
  472.4 21.1 %fusion.41 = f32[2,8192,384]{2,1,0:T(8,128)} fusion(bf16[2,384,384]{2,1,0:T(8,128)(2,1)S(1)} %bitcast.163, f32[8192,2,384]{0,2,1:T(8,128)} %bitcast.152, f32[2,384]{1,0:T(2,128)S(1)} %mul.196, f32[8192]{0:T(1024)S(1)} %fusion.46), kind=kOutput, calls=%fused_computation.57 | convolution fusion | flops 4850712576 | bytes 50957312 | tf_op jit(solution)/shard_map/rki,kij->rkj/dot_general | solution.py:19
  493.5 206.3 %all-to-all-done.1 = bf16[1,128,64,768]{3,2,0,1:T(8,128)(2,1)} async-done(((bf16[1,128,64,768]{3,2,0,1:T(8,128)(2,1)}), bf16[1,128,64,768]{3,2,0,1:T(8,128)(2,1)}, u32[]{:S(2)}, u32[]{:S(2)}) %all-to-all-start.1) | async-done | bytes 12582944 | tf_op jit(solution)/shard_map/all_to_all | solution.py:43
  699.8 7.4 convert_bitcast_fusion.2
  707.2 9.3 copy.114
  716.6 30.3 %reshape.272 = f32[8192,2,384]{2,1,0:T(2,128)} reshape(f32[1,32,4,64,768]{4,3,2,1,0:T(8,128)} %copy.114) | data formatting | bytes 50331648 | tf_op jit(solution)/shard_map/convert_element_type | solution.py:78
  746.9 39.9 %fusion.13 = (bf16[8192,2,384]{2,0,1:T(8,128)(2,1)}, bf16[8192,2,384]{2,0,1:T(8,128)(2,1)}, bf16[8192,2,384]{2,0,1:T(8,128)(2,1)}) fusion(f32[2,8192,384]{2,1,0:T(8,128)} %fusion.41, f32[8192,2,384]{2,1,0:T(2,128)} %reshape.272, bf16[2,384,384]{2,1,0:T(8,128)(2,1)S(1)} %bitcast.149, bf16[8192,2,384]{2,1,0:T(2,128)(2,1)} %reshape_reshape.4), kind=kOutput, calls=%fused_computation.23 | convolution fusion | flops 4932501504 | bytes 101253120 | tf_op jit(solution)/shard_map/rkj,kij->rki/dot_general | solution.py:27
  786.8 16.2 copy.123
  803.0 11.9 copy.144
  814.9 18.3 %copy.124 = bf16[1,32,256,768]{3,1,0,2:T(8,128)(2,1)} copy(bf16[1,32,256,768]{2,1,3,0:T(8,128)(2,1)} %bitcast.160) | data formatting | bytes 25165824 | tf_op jit(solution)/shard_map/convert_element_type | solution.py:83
  833.1 9.6 all-to-all-start.2
  842.7 0.1 copy.127
  842.8 269.4 %all-to-all-done.2 = bf16[1,32,256,768]{3,1,0,2:T(8,128)(2,1)} async-done(((bf16[1,32,256,768]{3,1,0,2:T(8,128)(2,1)}), bf16[1,32,256,768]{3,1,0,2:T(8,128)(2,1)}, u32[]{:S(2)}, u32[]{:S(2)}) %all-to-all-start.2) | async-done | bytes 12582944 | tf_op jit(solution)/shard_map/all_to_all | solution.py:39
  1112.2 9.0 copy.125
  1121.2 9.2 convert_bitcast_fusion.1
  1130.4 10.1 copy.126
  1140.5 0.0 copy-start.17
  1140.5 6.1 fusion.8
  1146.6 22.8 %convert_bitcast_fusion.3 = bf16[1,128,64,768]{1,3,2,0:T(8,128)(2,1)} fusion(bf16[128,64,768]{2,1,0:T(8,128)(2,1)} %fusion.8, bf16[128,128]{1,0:T(8,128)(2,1)S(1)} %copy-done.17), kind=kOutput, calls=%fused_computation.49 | convolution fusion | flops 1616904192 | bytes 25198592 | tf_op jit(solution)/shard_map/ip,bijd->bpjd/dot_general | solution.py:99
  1169.4 16.7 %copy.129 = bf16[1,128,64,768]{3,2,0,1:T(8,128)(2,1)} copy(bf16[1,128,64,768]{1,3,2,0:T(8,128)(2,1)} %convert_bitcast_fusion.3) | data formatting | bytes 25165824 | tf_op jit(solution)/shard_map/convert_element_type | solution.py:101
  1186.1 9.4 all-to-all-start.3
  1195.5 13.9 fusion.32
  1209.5 0.0 copy-start.5
  1209.5 15.7 fusion.40
  1225.2 1.6 pad_maximum_fusion
  1226.8 0.0 reduce-scatter.2.cloned.1.call-update
  1226.8 0.0 all-reduce.2.cloned.1.call-start
  1226.8 14.6 fusion.48
  1241.5 204.8 %reduce-scatter.2.cloned.1.call-done = f32[384,384]{1,0:T(8,128)} async-done(((f32[1536,384]{1,0:T(8,128)}), f32[384,384]{1,0:T(8,128)}) %reduce-scatter.2.cloned.1.call-update) | async-done | bytes 589840 | tf_op jit(solution)/shard_map/reduce_scatter | solution.py:108
  1446.3 0.0 all-reduce.2.cloned.1.call-update
  1446.3 14.7 fusion.47
  1460.9 24.8 %copy.134 = f32[8192,768]{1,0:T(8,128)} copy(f32[8192,768]{0,1:T(8,128)} %bitcast.150) | data formatting | bytes 50331648 | tf_op jit(solution)/shard_map/reshape | solution.py:28
  1485.7 24.7 %copy.133 = f32[1,8192,768]{2,1,0:T(8,128)} copy(f32[1,8192,768]{1,2,0:T(8,128)} %bitcast.151) | data formatting | bytes 50331648 | tf_op jit(solution)/shard_map/reshape | solution.py:28
  1510.4 24.7 %copy.119 = f32[1,8192,768]{2,1,0:T(8,128)} copy(f32[1,8192,768]{1,2,0:T(8,128)} %bitcast.155) | data formatting | bytes 50331648 | tf_op jit(solution)/shard_map/reshape | solution.py:20
  1535.1 1.9 broadcast_multiply_fusion
  1537.0 0.0 all-to-all-done.3
  1537.0 7.4 convert_bitcast_fusion
  1544.5 0.0 copy-start.7
  1544.5 0.0 copy-start.9
  1544.5 9.3 copy.131
  1553.8 15.5 fusion.23
  1569.3 20.7 %fusion.4 = f32[8192]{0:T(1024)S(1)} fusion(f32[8192,768]{1,0:T(8,128)} %copy.134, f32[32,768,256]{1,2,0:T(8,128)} %fusion.23, bf16[1,8192,768]{2,1,0:T(8,128)(2,1)} %param.9, f32[768]{0:T(1024)S(1)} %copy-done.19), kind=kLoop, calls=%fused_computation.6 | loop fusion | flops 31449088 | bytes 62950400 | tf_op jit(solution)/shard_map/transpose(jvp())/reduce_sum | solution.py:12
  1590.0 41.1 %fusion.1 = (bf16[1,8192,768]{2,1,0:T(8,128)(2,1)}, bf16[1,8192,768]{2,1,0:T(8,128)(2,1)}) fusion(f32[1,8192,768]{2,1,0:T(8,128)} %copy.133, f32[32,768,256]{1,2,0:T(8,128)} %fusion.23, bf16[1,8192,768]{2,1,0:T(8,128)(2,1)} %param.17, bf16[1,8192,768]{2,1,0:T(8,128)(2,1)} %param.9, f32[8192]{0:T(1024)S(1)} %multiply_multiply_fusion, f32[8192]{0:T(1024)S(1)} %copy-done.3, ...), kind=kLoop, calls=%fused_computation.2 | loop fusion | flops 75497472 | bytes 125897728 | tf_op jit(solution)/shard_map/convert_element_type | solution.py:107
  (33 shorter events, 0.1 us)
Async XLA Ops:
  7.2 739.7 %copy-start = (bf16[768,384]{1,0:T(8,128)(2,1)S(1)}, bf16[768,384]{1,0:T(8,128)(2,1)}, u32[]{:S(2)}) copy-start(bf16[768,384]{1,0:T(8,128)(2,1)} %param.16) | copy-start | bytes 1769476
  14.4 14.4 copy-start.10
  28.7 443.7 %copy-start.1 = (f32[8192]{0:T(1024)}, f32[8192]{0:T(1024)S(1)}, u32[]{:S(2)}) copy-start(f32[8192]{0:T(1024)S(1)} %fusion.46) | copy-start | bytes 98308
  28.7 24.8 %copy-start.6 = (f32[32,256]{1,0:T(8,128)S(1)}, f32[32,256]{1,0:T(8,128)}, u32[]{:S(2)}) copy-start(f32[32,256]{1,0:T(8,128)} %param.12) | copy-start | bytes 98308
  28.7 24.8 %copy-start.8 = (bf16[256,256]{1,0:T(8,128)(2,1)S(1)}, bf16[256,256]{1,0:T(8,128)(2,1)}, u32[]{:S(2)}) copy-start(bf16[256,256]{1,0:T(8,128)(2,1)} %param.11) | copy-start | bytes 393220
  28.7 24.7 %copy-start.18 = (f32[768]{0:T(1024)S(1)}, f32[768]{0:T(1024)}, u32[]{:S(2)}) copy-start(f32[768]{0:T(1024)} %param.10) | copy-start | bytes 9220
  359.9 21.7 %copy-start.12 = (f32[128,64]{0,1:T(8,128)S(1)}, f32[128,64]{0,1:T(8,128)}, u32[]{:S(2)}) copy-start(f32[128,64]{0,1:T(8,128)} %param.14) | copy-start | bytes 98308
  359.9 21.7 %copy-start.16 = (bf16[128,128]{1,0:T(8,128)(2,1)S(1)}, bf16[128,128]{1,0:T(8,128)(2,1)}, u32[]{:S(2)}) copy-start(bf16[128,128]{1,0:T(8,128)(2,1)} %param.13) | copy-start | bytes 98308
  422.3 277.5 %all-to-all-start.1 = ((bf16[1,128,64,768]{3,2,0,1:T(8,128)(2,1)}), bf16[1,128,64,768]{3,2,0,1:T(8,128)(2,1)}, u32[]{:S(2)}, u32[]{:S(2)}) async-start(bf16[1,128,64,768]{3,2,0,1:T(8,128)(2,1)} %copy.112), calls=%async_computation.1 | async-start | bytes 25165824 | tf_op jit(solution)/shard_map/all_to_all | solution.py:43
  430.3 42.0 %copy-start.14 = (f32[2,384]{1,0:T(2,128)}, f32[2,384]{1,0:T(2,128)S(1)}, u32[]{:S(2)}) copy-start(f32[2,384]{1,0:T(2,128)S(1)} %mul.196) | copy-start | bytes 9220
  430.3 42.0 %copy-start.4 = (bf16[768,384]{1,0:T(8,128)(2,1)S(1)}, bf16[768,384]{1,0:T(8,128)(2,1)}, u32[]{:S(2)}) copy-start(bf16[768,384]{1,0:T(8,128)(2,1)} %param.15) | copy-start | bytes 1769476
  814.9 27.8 %copy-start.13 = (f32[128,64]{0,1:T(8,128)S(1)}, f32[128,64]{0,1:T(8,128)}, u32[]{:S(2)}) copy-start(f32[128,64]{0,1:T(8,128)} %param.14) | copy-start | bytes 98308
  833.1 279.0 %all-to-all-start.2 = ((bf16[1,32,256,768]{3,1,0,2:T(8,128)(2,1)}), bf16[1,32,256,768]{3,1,0,2:T(8,128)(2,1)}, u32[]{:S(2)}, u32[]{:S(2)}) async-start(bf16[1,32,256,768]{3,1,0,2:T(8,128)(2,1)} %copy.124), calls=%async_computation.2 | async-start | bytes 25165824 | tf_op jit(solution)/shard_map/all_to_all | solution.py:39
  1140.5 6.1 copy-start.17
  1186.1 350.9 %all-to-all-start.3 = ((bf16[1,128,64,768]{3,2,0,1:T(8,128)(2,1)}), bf16[1,128,64,768]{3,2,0,1:T(8,128)(2,1)}, u32[]{:S(2)}, u32[]{:S(2)}) async-start(bf16[1,128,64,768]{3,2,0,1:T(8,128)(2,1)} %copy.129), calls=%async_computation.3 | async-start | bytes 25165824 | tf_op jit(solution)/shard_map/all_to_all | solution.py:43
  1195.5 250.7 %reduce-scatter.2.cloned.1.call-start = ((), (), s32[]{:S(2)}) async-start(), calls=%async_computation.5 | async-start | bytes 2949120 | tf_op jit(solution)/shard_map/reduce_scatter | solution.py:108
  1195.5 14.0 copy-start.2
  1195.5 14.0 copy-start.15
  1209.5 17.4 %copy-start.5 = (bf16[768,384]{1,0:T(8,128)(2,1)S(1)}, bf16[768,384]{1,0:T(8,128)(2,1)}, u32[]{:S(2)}) copy-start(bf16[768,384]{1,0:T(8,128)(2,1)} %param.15) | copy-start | bytes 1769476
  1226.8 308.3 %all-reduce.2.cloned.1.call-start = ((), (), s32[]{:S(2)}) async-start(), calls=%async_computation.6 | async-start | bytes 1179648 | tf_op jit(solution)/shard_map/psum | solution.py:109
  1544.5 9.3 copy-start.7
  1544.5 9.3 copy-start.9
  1553.8 15.5 copy-start.19
  1569.3 20.7 %copy-start.11 = (f32[8192]{0:T(1024)S(1)}, f32[8192]{0:T(1024)}, u32[]{:S(2)}) copy-start(f32[8192]{0:T(1024)} %copy-done.10) | copy-start | bytes 98308
  1569.3 20.7 %copy-start.3 = (f32[8192]{0:T(1024)S(1)}, f32[8192]{0:T(1024)}, u32[]{:S(2)}) copy-start(f32[8192]{0:T(1024)} %copy-done.1) | copy-start | bytes 98308
Sparse Core Ops, SparseCore 0:
  1226.9 219.3 reduce-scatter.1
  1448.6 32.5 all-reduce.1
where the time goes:
time: 1650 us; the launch traced here: 1640 us
  waiting for transfers between devices  680 us (41%)
  local copies, waits for them, and re-layouts  327 us (20%)
  blocking collectives  276 us (17%)
  matrix products  197 us (12%)
  other arithmetic  117 us (7%)
  starting transfers between devices  27 us (2%)
    all_to_all x1, blocking collectives, to_columns(): lax.all_to_all(row_layout, 'seq', split_axis=2, concat_axis=1, tiled=True)  276 us
    all_to_all x1, waiting for transfers between devices, to_columns(): lax.all_to_all(row_layout, 'seq', split_axis=2, concat_axis=1, tiled=True)  269 us
    all_to_all x2, waiting for transfers between devices, to_rows(): lax.all_to_all(col_layout, 'seq', split_axis=1, concat_axis=2, tiled=True)  206 us
    reduce_scatter x1, waiting for transfers between devices, shards(): lax.psum_scatter(weight_term, 'seq', scatter_dimension=0, tiled=True)  205 us
    dot_general x2, matrix products, block_back(): jnp.einsum('rkj,kij->rki', grouped, stacked, preferred_element_type=jnp.f...  54.5 us
    reshape x2, local copies, waits for them, and re-layouts, block_back(): return result.reshape(partner.shape[0], -1)  49.5 us
    convert_element_type x2, local copies, waits for them, and re-layouts, shards(): inputs_wide = inputs.reshape(flat_rows, channels).astype(jnp.float32)  42.4 us
    convert_element_type x1, other arithmetic, shards(): (cotan_rows.astype(jnp.float32) + pullback(act_grad)[0]).astype(jnp.bfloa...  41.1 us
  transfers between devices with their start and end apart: 5, of which 3 were waited for; matrix products, arithmetic and copies ran while one was open for 12% of the time, Pallas kernels for 0%

commit v1 on v0

--- a/solution.py
+++ b/solution.py
@@ -5,6 +5,12 @@
 from jax.sharding import PartitionSpec as P
 
 norm_eps = 1e-06
+
+
+def stacked_exchange(x, name, split, join):
+    cells = jnp.split(x, lax.axis_size(name), axis=split)
+    received = lax.all_to_all(jnp.stack(cells), name, 0, 0)
+    return jnp.concatenate(received, axis=join)
 
 
 def normalize(values, norm_gain):
@@ -36,7 +42,7 @@
 
 
 def to_columns(row_layout):
-    return lax.all_to_all(row_layout, "seq", split_axis=2, concat_axis=1, tiled=True)
+    return stacked_exchange(row_layout, "seq", 2, 1)
 
 
 def to_rows(col_layout):

time: 1650 us -> 1610 us (0.976)
  local copies, waits for them, and re-layouts: 327 us -> 267 us
  other arithmetic: 117 us -> 137 us
    another operation x0 -> x3, local copies, waits for them, and re-layouts: none -> 43.7 us  [stacked_exchange(): received = lax.all_to_all(jnp.stack(cells), name, 0, 0)]
    all_to_all x3 -> x0, local copies, waits for them, and re-layouts: 30.7 us -> none  [to_columns(): lax.all_to_all(row_layout, 'seq', split_axis=2, concat_axis=1, tiled=True)]
    convert_element_type x2 -> x0, local copies, waits for them, and re-layouts: 26.6 us -> none  [the longest x1 16.6 us: shards(): mixed_rows = (inner_out * twiddle[None, :, :, None]).astype(jnp.bfloat16)]
    convert_element_type x2 -> x1, local copies, waits for them, and re-layouts: 42.4 us -> 17.6 us  [shards(): inputs_wide = inputs.reshape(flat_rows, channels).astype(jnp.float32)]
    another operation x0 -> x2, other arithmetic: none -> 23.9 us  [stacked_exchange(): received = lax.all_to_all(jnp.stack(cells), name, 0, 0)]
    convert_element_type x2 -> x1, local copies, waits for them, and re-layouts: 34.4 us -> 16.8 us  [shards(): mix_grad = (back_gated * gate_pre * gate_sig).astype(jnp.bfloat16)]
  transfers between devices with their start and end apart: 5 -> 5, of which waited for: 3 -> 3; matrix products, arithmetic and copies ran while one was open for 12% -> 13% of each run, Pallas kernels for 0% -> 0%
where the time goes in v1:
time: 1610 us; the launch traced here: 1600 us
  waiting for transfers between devices  680 us (42%)
  blocking collectives  276 us (17%)
  local copies, waits for them, and re-layouts  267 us (17%)
  matrix products  197 us (12%)
  other arithmetic  137 us (9%)
  starting transfers between devices  27 us (2%)
    all_to_all x1, blocking collectives, stacked_exchange(): received = lax.all_to_all(jnp.stack(cells), name, 0, 0)  276 us
    all_to_all x1, waiting for transfers between devices, stacked_exchange(): received = lax.all_to_all(jnp.stack(cells), name, 0, 0)  269 us
    all_to_all x2, waiting for transfers between devices, to_rows(): lax.all_to_all(col_layout, 'seq', split_axis=1, concat_axis=2, tiled=True)  206 us
    reduce_scatter x1, waiting for transfers between devices, shards(): lax.psum_scatter(weight_term, 'seq', scatter_dimension=0, tiled=True)  204 us
    dot_general x2, matrix products, block_back(): jnp.einsum('rkj,kij->rki', grouped, stacked, preferred_element_type=jnp.f...  54.7 us
    reshape x2, local copies, waits for them, and re-layouts, block_back(): return result.reshape(partner.shape[0], -1)  49.5 us
    another operation x3, local copies, waits for them, and re-layouts, stacked_exchange(): received = lax.all_to_all(jnp.stack(cells), name, 0, 0)  43.7 us
    convert_element_type x1, other arithmetic, shards(): (cotan_rows.astype(jnp.float32) + pullback(act_grad)[0]).astype(jnp.bfloa...  41.1 us
  transfers between devices with their start and end apart: 5, of which 3 were waited for; matrix products, arithmetic and copies ran while one was open for 13% of the time, Pallas kernels for 0%

profile of v1, /device:TPU:21, one launch (start us, length us, event | category | flops | bytes accessed | tf_op | source)
XLA Modules:
  0.0 1598.0 jit_solution(15134747082382316010)
XLA Ops:
  7.2 0.0 copy-start
  7.2 7.2 fusion.21
  14.4 0.0 copy-start.10
  14.4 0.0 copy-start.6
  14.4 0.0 copy-start.8
  14.4 0.0 copy-start.18
  14.4 14.3 convert_element_type.129
  28.8 0.0 copy-done.6
  28.8 0.0 copy-done.8
  28.8 0.0 copy-done.18
  28.8 13.8 fusion.24
  42.6 5.4 slice_bitcast_fusion.7
  48.1 1.7 pad_maximum_fusion.1
  49.7 0.0 copy-start.12
  49.8 0.0 copy-start.16
  49.8 275.6 %all_to_all.28 = bf16[4,1,32,64,768]{4,3,2,1,0:T(8,128)(2,1)} all-to-all(bf16[4,1,32,64,768]{4,3,2,1,0:T(8,128)(2,1)S(1)} %pad_maximum_fusion.1), channel_id=1, replica_groups=mesh['groups'=2,'seq'=4,'dp'=4] {'seq'}, dimensions={0} | all-to-all | bytes 25165824 | tf_op jit(solution)/shard_map/all_to_all | solution.py:12
  325.4 24.2 %fusion.8 = bf16[1,128,64,768]{1,3,2,0:T(8,128)(2,1)} fusion(f32[128,64]{0,1:T(8,128)S(1)} %copy-done.12, bf16[128,64,768]{2,1,0:T(8,128)(2,1)} %bitcast.168, bf16[128,128]{1,0:T(8,128)(2,1)S(1)} %copy-done.16), kind=kOutput, calls=%fused_computation.16 | convolution fusion | flops 1623195648 | bytes 25231360 | tf_op jit(solution)/shard_map/ip,bpjd->bijd/dot_general | solution.py:79
  349.6 16.5 %copy.76 = bf16[1,128,64,768]{3,2,0,1:T(8,128)(2,1)} copy(bf16[1,128,64,768]{1,3,2,0:T(8,128)(2,1)} %fusion.8) | data formatting | bytes 25165824 | tf_op jit(solution)/shard_map/convert_element_type | solution.py:80
  366.1 8.0 all-to-all-start.1
  374.1 0.0 copy-start.14
  374.2 17.6 %copy.107 = f32[1,8192,768]{1,2,0:T(8,128)} copy(bf16[1,8192,768]{2,1,0:T(8,128)(2,1)} %param.9) | data formatting | bytes 37748736 | tf_op jit(solution)/shard_map/convert_element_type | solution.py:71
  391.8 24.4 %reshape_reshape.4 = bf16[8192,2,384]{2,1,0:T(2,128)(2,1)} reshape(bf16[1,8192,768]{2,1,0:T(8,128)(2,1)} %param.17) | data formatting | bytes 25165824 | tf_op jit(solution)/shard_map/reshape;reshape | solution.py:31
  416.2 0.0 copy-done.4
  416.2 21.1 %fusion.41 = f32[2,8192,384]{2,1,0:T(8,128)} fusion(bf16[2,384,384]{2,1,0:T(8,128)(2,1)S(1)} %bitcast.171, f32[8192,2,384]{0,2,1:T(8,128)} %bitcast.162, f32[2,384]{1,0:T(2,128)S(1)} %mul.196, f32[8192]{0:T(1024)S(1)} %fusion.46), kind=kOutput, calls=%fused_computation.62 | convolution fusion | flops 4850712576 | bytes 50957312 | tf_op jit(solution)/shard_map/rki,kij->rkj/dot_general | solution.py:25
  437.3 206.3 %all-to-all-done.1 = bf16[1,128,64,768]{3,2,0,1:T(8,128)(2,1)} async-done(((bf16[1,128,64,768]{3,2,0,1:T(8,128)(2,1)}), bf16[1,128,64,768]{3,2,0,1:T(8,128)(2,1)}, u32[]{:S(2)}, u32[]{:S(2)}) %all-to-all-start.1) | async-done | bytes 12582944 | tf_op jit(solution)/shard_map/all_to_all | solution.py:49
  643.6 7.4 convert_bitcast_fusion.1
  651.0 9.3 copy.78
  660.3 30.3 %reshape.272 = f32[8192,2,384]{2,1,0:T(2,128)} reshape(f32[1,32,4,64,768]{4,3,2,1,0:T(8,128)} %copy.78) | data formatting | bytes 50331648 | tf_op jit(solution)/shard_map/convert_element_type | solution.py:84
  690.6 39.8 %fusion.13 = (bf16[8192,2,384]{2,0,1:T(8,128)(2,1)}, bf16[8192,2,384]{2,0,1:T(8,128)(2,1)}, bf16[8192,2,384]{2,0,1:T(8,128)(2,1)}) fusion(f32[2,8192,384]{2,1,0:T(8,128)} %fusion.41, f32[8192,2,384]{2,1,0:T(2,128)} %reshape.272, bf16[2,384,384]{2,1,0:T(8,128)(2,1)S(1)} %bitcast.159, bf16[8192,2,384]{2,1,0:T(2,128)(2,1)} %reshape_reshape.4), kind=kOutput, calls=%fused_computation.23 | convolution fusion | flops 4932501504 | bytes 101253120 | tf_op jit(solution)/shard_map/rkj,kij->rki/dot_general | solution.py:33
  730.4 16.8 %copy.87 = bf16[8192,2,384]{0,2,1:T(8,128)(2,1)} copy(bf16[8192,2,384]{2,0,1:T(8,128)(2,1)} %get-tuple-element.3) | data formatting | bytes 25165824 | tf_op jit(solution)/shard_map/convert_element_type | solution.py:89
  747.2 8.1 copy.110
  755.3 9.9 slice_bitcast_fusion.3
  765.2 22.2 %pad_maximum_fusion = bf16[4,1,32,64,768]{3,2,4,1,0:T(8,128)(2,1)} fusion(bf16[1,1,32,64,768]{3,2,4,1,0:T(8,128)(2,1)} %get-tuple-element.9, bf16[1,1,32,64,768]{3,2,4,1,0:T(8,128)(2,1)} %get-tuple-element.10, bf16[1,1,32,64,768]{3,2,4,1,0:T(8,128)(2,1)} %get-tuple-element.11, bf16[1,1,32,64,768]{3,2,4,1,0:T(8,128)(2,1)} %get-tuple-element.8), kind=kLoop, calls=%fused_computation.3 | loop fusion | flops 18874368 | bytes 25165824 | tf_op jit(solution)/shard_map/stack | solution.py:12
  787.4 28.4 %copy.90 = bf16[4,1,32,64,768]{4,3,2,1,0:T(8,128)(2,1)} copy(bf16[4,1,32,64,768]{3,2,4,1,0:T(8,128)(2,1)} %pad_maximum_fusion) | data formatting | bytes 25165824 | tf_op jit(solution)/shard_map/stack | solution.py:12
  815.8 9.5 all-to-all-start.2
  825.4 0.1 copy.92
  825.5 0.0 copy-start.17
  825.5 269.4 %all-to-all-done.2 = bf16[4,1,32,64,768]{4,3,2,1,0:T(8,128)(2,1)} async-done(((bf16[4,1,32,64,768]{4,3,2,1,0:T(8,128)(2,1)}), bf16[4,1,32,64,768]{4,3,2,1,0:T(8,128)(2,1)}, u32[]{:S(2)}, u32[]{:S(2)}) %all-to-all-start.2) | async-done | bytes 12582944 | tf_op jit(solution)/shard_map/all_to_all | solution.py:12
  1094.8 11.6 fusion.7
  1106.4 22.8 %convert_bitcast_fusion.2 = bf16[1,128,64,768]{1,3,2,0:T(8,128)(2,1)} fusion(bf16[128,64,768]{2,1,0:T(8,128)(2,1)} %fusion.7, bf16[128,128]{1,0:T(8,128)(2,1)S(1)} %copy-done.17), kind=kOutput, calls=%fused_computation.50 | convolution fusion | flops 1616904192 | bytes 25198592 | tf_op jit(solution)/shard_map/ip,bijd->bpjd/dot_general | solution.py:105
  1129.2 16.5 %copy.94 = bf16[1,128,64,768]{3,2,0,1:T(8,128)(2,1)} copy(bf16[1,128,64,768]{1,3,2,0:T(8,128)(2,1)} %convert_bitcast_fusion.2) | data formatting | bytes 25165824 | tf_op jit(solution)/shard_map/convert_element_type | solution.py:107
  1145.7 9.4 all-to-all-start.3
  1155.1 14.1 fusion.32
  1169.3 0.0 copy-start.5
  1169.3 15.7 fusion.40
  1185.0 1.6 pad_maximum_fusion.2
  1186.6 0.0 reduce-scatter.2.cloned.1.call-update
  1186.6 0.0 all-reduce.2.cloned.1.call-start
  1186.6 14.9 fusion.48
  1201.5 204.3 %reduce-scatter.2.cloned.1.call-done = f32[384,384]{1,0:T(8,128)} async-done(((f32[1536,384]{1,0:T(8,128)}), f32[384,384]{1,0:T(8,128)}) %reduce-scatter.2.cloned.1.call-update) | async-done | bytes 589840 | tf_op jit(solution)/shard_map/reduce_scatter | solution.py:114
  1405.8 0.0 all-reduce.2.cloned.1.call-update
  1405.9 14.7 fusion.47
  1420.5 24.8 %copy.99 = f32[8192,768]{1,0:T(8,128)} copy(f32[8192,768]{0,1:T(8,128)} %bitcast.160) | data formatting | bytes 50331648 | tf_op jit(solution)/shard_map/reshape | solution.py:34
  1445.3 24.7 %copy.98 = f32[1,8192,768]{2,1,0:T(8,128)} copy(f32[1,8192,768]{1,2,0:T(8,128)} %bitcast.161) | data formatting | bytes 50331648 | tf_op jit(solution)/shard_map/reshape | solution.py:34
  1470.0 24.7 %copy.83 = f32[1,8192,768]{2,1,0:T(8,128)} copy(f32[1,8192,768]{1,2,0:T(8,128)} %bitcast.165) | data formatting | bytes 50331648 | tf_op jit(solution)/shard_map/reshape | solution.py:26
  1494.7 1.9 broadcast_multiply_fusion
  1496.6 0.0 all-to-all-done.3
  1496.6 7.4 convert_bitcast_fusion
  1504.0 0.0 copy-start.7
  1504.1 0.0 copy-start.9
  1504.1 9.3 copy.96
  1513.3 15.5 fusion.23
  1528.9 20.7 %fusion.4 = f32[8192]{0:T(1024)S(1)} fusion(f32[8192,768]{1,0:T(8,128)} %copy.99, f32[32,768,256]{1,2,0:T(8,128)} %fusion.23, bf16[1,8192,768]{2,1,0:T(8,128)(2,1)} %param.9, f32[768]{0:T(1024)S(1)} %copy-done.19), kind=kLoop, calls=%fused_computation.7 | loop fusion | flops 31449088 | bytes 62950400 | tf_op jit(solution)/shard_map/transpose(jvp())/reduce_sum | solution.py:18
  1549.6 41.1 %fusion.1 = (bf16[1,8192,768]{2,1,0:T(8,128)(2,1)}, bf16[1,8192,768]{2,1,0:T(8,128)(2,1)}) fusion(f32[1,8192,768]{2,1,0:T(8,128)} %copy.98, f32[32,768,256]{1,2,0:T(8,128)} %fusion.23, bf16[1,8192,768]{2,1,0:T(8,128)(2,1)} %param.17, bf16[1,8192,768]{2,1,0:T(8,128)(2,1)} %param.9, f32[8192]{0:T(1024)S(1)} %multiply_multiply_fusion, f32[8192]{0:T(1024)S(1)} %copy-done.3, ...), kind=kLoop, calls=%fused_computation.2 | loop fusion | flops 75497472 | bytes 125897728 | tf_op jit(solution)/shard_map/convert_element_type | solution.py:113
  (30 shorter events, 0.1 us)
Async XLA Ops:
  7.2 683.5 %copy-start = (bf16[768,384]{1,0:T(8,128)(2,1)S(1)}, bf16[768,384]{1,0:T(8,128)(2,1)}, u32[]{:S(2)}) copy-start(bf16[768,384]{1,0:T(8,128)(2,1)} %param.16) | copy-start | bytes 1769476
  14.4 14.4 copy-start.10
  14.4 14.4 copy-start.6
  14.4 14.4 copy-start.8
  14.4 14.4 copy-start.18
  28.7 387.4 %copy-start.1 = (f32[8192]{0:T(1024)}, f32[8192]{0:T(1024)S(1)}, u32[]{:S(2)}) copy-start(f32[8192]{0:T(1024)S(1)} %fusion.46) | copy-start | bytes 98308
  49.7 275.6 %copy-start.12 = (f32[128,64]{0,1:T(8,128)S(1)}, f32[128,64]{0,1:T(8,128)}, u32[]{:S(2)}) copy-start(f32[128,64]{0,1:T(8,128)} %param.14) | copy-start | bytes 98308
  49.8 275.6 %copy-start.16 = (bf16[128,128]{1,0:T(8,128)(2,1)S(1)}, bf16[128,128]{1,0:T(8,128)(2,1)}, u32[]{:S(2)}) copy-start(bf16[128,128]{1,0:T(8,128)(2,1)} %param.13) | copy-start | bytes 98308
  366.1 277.5 %all-to-all-start.1 = ((bf16[1,128,64,768]{3,2,0,1:T(8,128)(2,1)}), bf16[1,128,64,768]{3,2,0,1:T(8,128)(2,1)}, u32[]{:S(2)}, u32[]{:S(2)}) async-start(bf16[1,128,64,768]{3,2,0,1:T(8,128)(2,1)} %copy.76), calls=%async_computation.1 | async-start | bytes 25165824 | tf_op jit(solution)/shard_map/all_to_all | solution.py:49
  374.1 42.0 %copy-start.14 = (f32[2,384]{1,0:T(2,128)}, f32[2,384]{1,0:T(2,128)S(1)}, u32[]{:S(2)}) copy-start(f32[2,384]{1,0:T(2,128)S(1)} %mul.196) | copy-start | bytes 9220
  391.8 24.4 %copy-start.4 = (bf16[768,384]{1,0:T(8,128)(2,1)S(1)}, bf16[768,384]{1,0:T(8,128)(2,1)}, u32[]{:S(2)}) copy-start(bf16[768,384]{1,0:T(8,128)(2,1)} %param.15) | copy-start | bytes 1769476
  815.8 9.5 copy-start.13
  815.8 279.0 %all-to-all-start.2 = ((bf16[4,1,32,64,768]{4,3,2,1,0:T(8,128)(2,1)}), bf16[4,1,32,64,768]{4,3,2,1,0:T(8,128)(2,1)}, u32[]{:S(2)}, u32[]{:S(2)}) async-start(bf16[4,1,32,64,768]{4,3,2,1,0:T(8,128)(2,1)} %copy.90), calls=%async_computation.2 | async-start | bytes 25165824 | tf_op jit(solution)/shard_map/all_to_all | solution.py:12
  825.5 281.0 %copy-start.17 = (bf16[128,128]{1,0:T(8,128)(2,1)S(1)}, bf16[128,128]{1,0:T(8,128)(2,1)}, u32[]{:S(2)}) copy-start(bf16[128,128]{1,0:T(8,128)(2,1)} %param.13) | copy-start | bytes 98308
  1145.7 350.9 %all-to-all-start.3 = ((bf16[1,128,64,768]{3,2,0,1:T(8,128)(2,1)}), bf16[1,128,64,768]{3,2,0,1:T(8,128)(2,1)}, u32[]{:S(2)}, u32[]{:S(2)}) async-start(bf16[1,128,64,768]{3,2,0,1:T(8,128)(2,1)} %copy.94), calls=%async_computation.3 | async-start | bytes 25165824 | tf_op jit(solution)/shard_map/all_to_all | solution.py:49
  1155.1 250.7 %reduce-scatter.2.cloned.1.call-start = ((), (), s32[]{:S(2)}) async-start(), calls=%async_computation.5 | async-start | bytes 2949120 | tf_op jit(solution)/shard_map/reduce_scatter | solution.py:114
  1155.1 14.1 copy-start.2
  1155.1 14.1 copy-start.15
  1169.3 17.3 %copy-start.5 = (bf16[768,384]{1,0:T(8,128)(2,1)S(1)}, bf16[768,384]{1,0:T(8,128)(2,1)}, u32[]{:S(2)}) copy-start(bf16[768,384]{1,0:T(8,128)(2,1)} %param.15) | copy-start | bytes 1769476
  1186.6 308.1 %all-reduce.2.cloned.1.call-start = ((), (), s32[]{:S(2)}) async-start(), calls=%async_computation.6 | async-start | bytes 1179648 | tf_op jit(solution)/shard_map/psum | solution.py:115
  1504.0 9.3 copy-start.7
  1504.1 9.3 copy-start.9
  1513.3 15.5 copy-start.19
  1528.8 20.7 %copy-start.11 = (f32[8192]{0:T(1024)S(1)}, f32[8192]{0:T(1024)}, u32[]{:S(2)}) copy-start(f32[8192]{0:T(1024)} %copy-done.10) | copy-start | bytes 98308
  1528.8 20.7 %copy-start.3 = (f32[8192]{0:T(1024)S(1)}, f32[8192]{0:T(1024)}, u32[]{:S(2)}) copy-start(f32[8192]{0:T(1024)} %copy-done.1) | copy-start | bytes 98308
Sparse Core Ops, SparseCore 0:
  1186.7 219.0 reduce-scatter.1
  1408.2 32.6 all-reduce.1
